TPU v7x, 32 devices: a whole 2x2x4 slice. The times are simulated.
32 devices in a mesh: gx: 8 (over z, core), gy: 4 (over y, x).
Axes of the slice: x: 2, y: 2, z: 4, core: 2. Of those that a mesh axis runs over, the one named last changes fastest.
Arguments:
- tokens: bfloat16 [64, 32, 8, 768], P('gx', 'gy'), may hold values from -64 to 64
- target: bfloat16 [64, 32, 8, 768], P('gx', 'gy'), may hold values from -4 to 4
- norm_gain: float32 [768], replicated, may hold values from 0.1 to 1.9
- qkv_weight: bfloat16 [768, 1152], P('gy'), may hold values from -4 to 4
- proj_weight: bfloat16 [384, 768], P('gy'), may hold values from -1.5 to 1.5
Outputs:
- block_out: bfloat16 [64, 32, 8, 768], P('gx', 'gy')
- qkv_grad: float32 [768, 1152], P('gy')
All inputs are finite; a program needn't handle non-finite values.
Results may differ from a plain program's by a relative error of at most 0.0094.
Values may be sent and summed in bfloat16 or wider, within the bound.
A program may use at most 64 MiB of HBM per device.

v0:
```python
import math

import jax
import jax.numpy as jnp
from jax import lax
from jax.sharding import PartitionSpec as P

HEADS = 12
HD = 32
WIN = 8


norm_eps = 1e-05


def shifted(x, axis, by):
    devices = lax.axis_size(axis)
    return lax.ppermute(x, axis, [(i, (i + by) % devices) for i in range(devices)])


def displace(volume, half_width):
    volume = jnp.roll(volume, -half_width, axis=2)
    upper_rows = shifted(volume[:half_width], "gx", -1)
    volume = jnp.concatenate([volume[half_width:], upper_rows], 0)
    upper_cols = shifted(volume[:, :half_width], "gy", -1)
    return jnp.concatenate([volume[:, half_width:], upper_cols], 1)


def restore(volume, half_width):
    lower_rows = shifted(volume[-half_width:], "gx", 1)
    volume = jnp.concatenate([lower_rows, volume[:-half_width]], 0)
    lower_cols = shifted(volume[:, -half_width:], "gy", 1)
    volume = jnp.concatenate([lower_cols, volume[:, :-half_width]], 1)
    return jnp.roll(volume, half_width, axis=2)


def into_windows(volume, window):
    ext_x, ext_y, ext_z, channels = volume.shape
    blocks = volume.reshape(ext_x, ext_y, ext_z // window, window, channels)
    return blocks.transpose(2, 0, 1, 3, 4).reshape(
        ext_z // window, ext_x * ext_y * window, channels
    )


def from_windows(windows, ext_x, ext_y, window):
    window_count = windows.shape[0]
    channels = windows.shape[2]
    blocks = windows.reshape(window_count, ext_x, ext_y, window, channels).transpose(1, 2, 0, 3, 4)
    return blocks.reshape(ext_x, ext_y, window_count * window, channels)


def head_probs(queries, keys_in, score_scale):
    scores = (
        jnp.einsum("wqd,wkd->wqk", queries, keys_in, preferred_element_type=jnp.float32)
        * score_scale
    )
    row_max = jnp.max(scores, -1, keepdims=True)
    exponent = jnp.exp(scores - row_max)
    return exponent / jnp.sum(exponent, -1, keepdims=True)


def shards(tokens, target, norm_gain, qkv_weight, proj_weight):
    window = WIN
    half_width = WIN // 2
    head_count = HEADS
    head_dim = HD
    inner_dim = HEADS * HD
    score_scale = HD ** (-0.5)
    ext_x, ext_y, ext_z, channels = tokens.shape
    total_tokens = ext_x * ext_y * ext_z * lax.axis_size("gx") * lax.axis_size("gy")
    loss_scale = 2.0 / math.sqrt(total_tokens)
    widened = tokens.astype(jnp.float32)
    token_mean = jnp.mean(widened, -1, keepdims=True)
    centred = widened - token_mean
    variance = jnp.mean(centred * centred, -1, keepdims=True)
    normed = (centred * lax.rsqrt(variance + norm_eps) * norm_gain).astype(jnp.bfloat16)
    windows_in = into_windows(displace(normed, half_width), window)
    window_count = windows_in.shape[0]
    window_tokens = windows_in.shape[1]
    flat_in = windows_in.reshape(-1, channels)
    qkv_whole = lax.all_gather(qkv_weight, "gy", axis=0, tiled=True)
    qkv_act = jnp.dot(flat_in, qkv_whole, preferred_element_type=jnp.float32).astype(jnp.bfloat16)
    qkv_act = qkv_act.reshape(window_count, window_tokens, 3 * inner_dim)

    def forward_head(head_idx, attn_buffer):
        queries = lax.dynamic_slice_in_dim(qkv_act, head_idx * head_dim, head_dim, 2)
        keys_in = lax.dynamic_slice_in_dim(qkv_act, inner_dim + head_idx * head_dim, head_dim, 2)
        values = lax.dynamic_slice_in_dim(qkv_act, 2 * inner_dim + head_idx * head_dim, head_dim, 2)
        attn_prob = head_probs(queries, keys_in, score_scale).astype(jnp.bfloat16)
        mixed = jnp.einsum(
            "wqk,wkd->wqd", attn_prob, values, preferred_element_type=jnp.float32
        ).astype(jnp.bfloat16)
        return lax.dynamic_update_slice_in_dim(attn_buffer, mixed, head_idx * head_dim, 2)

    attn_out = lax.fori_loop(
        0,
        head_count,
        forward_head,
        jnp.zeros((window_count, window_tokens, inner_dim), jnp.bfloat16),
    )
    proj_whole = lax.all_gather(proj_weight, "gy", axis=0, tiled=True)
    contract_cols = (((1,), (1,)), ((), ()))
    block_shift = jnp.dot(
        attn_out.reshape(-1, inner_dim), proj_whole, preferred_element_type=jnp.float32
    ).astype(jnp.bfloat16)
    block_shift = block_shift.reshape(window_count, window_tokens, channels)
    block_out = restore(from_windows(block_shift, ext_x, ext_y, window), half_width)
    grad_out = ((block_out.astype(jnp.float32) - target.astype(jnp.float32)) * loss_scale).astype(
        jnp.bfloat16
    )
    grad_shift = into_windows(displace(grad_out, half_width), window)
    grad_windows = lax.dot_general(
        grad_shift.reshape(-1, channels),
        proj_whole,
        contract_cols,
        preferred_element_type=jnp.float32,
    ).astype(jnp.bfloat16)
    grad_windows = grad_windows.reshape(window_count, window_tokens, inner_dim)

    def backward_head(head_idx, grad_buffer):
        queries = lax.dynamic_slice_in_dim(qkv_act, head_idx * head_dim, head_dim, 2)
        keys_in = lax.dynamic_slice_in_dim(qkv_act, inner_dim + head_idx * head_dim, head_dim, 2)
        values = lax.dynamic_slice_in_dim(qkv_act, 2 * inner_dim + head_idx * head_dim, head_dim, 2)
        attn_prob = head_probs(queries, keys_in, score_scale)
        prob_half = attn_prob.astype(jnp.bfloat16)
        grad_mixed = lax.dynamic_slice_in_dim(grad_windows, head_idx * head_dim, head_dim, 2)
        grad_probs = jnp.einsum(
            "wqd,wkd->wqk", grad_mixed, values, preferred_element_type=jnp.float32
        )
        grad_values = jnp.einsum(
            "wqk,wqd->wkd", prob_half, grad_mixed, preferred_element_type=jnp.float32
        ).astype(jnp.bfloat16)
        row_dot = jnp.sum(grad_probs * attn_prob, -1, keepdims=True)
        grad_scores = (attn_prob * (grad_probs - row_dot)).astype(jnp.bfloat16)
        grad_queries = (
            jnp.einsum("wqk,wkd->wqd", grad_scores, keys_in, preferred_element_type=jnp.float32)
            * score_scale
        ).astype(jnp.bfloat16)
        grad_keys = (
            jnp.einsum("wqk,wqd->wkd", grad_scores, queries, preferred_element_type=jnp.float32)
            * score_scale
        ).astype(jnp.bfloat16)
        grad_buffer = lax.dynamic_update_slice_in_dim(
            grad_buffer, grad_queries, head_idx * head_dim, 2
        )
        grad_buffer = lax.dynamic_update_slice_in_dim(
            grad_buffer, grad_keys, inner_dim + head_idx * head_dim, 2
        )
        return lax.dynamic_update_slice_in_dim(
            grad_buffer, grad_values, 2 * inner_dim + head_idx * head_dim, 2
        )

    grad_qkv = lax.fori_loop(
        0,
        head_count,
        backward_head,
        jnp.zeros((window_count, window_tokens, 3 * inner_dim), jnp.bfloat16),
    )
    grad_flat = grad_qkv.reshape(-1, 3 * inner_dim)
    contract_rows = (((0,), (0,)), ((), ()))
    shard_rows = qkv_weight.shape[0]
    local_grad = lax.dot_general(
        flat_in, grad_flat, contract_rows, preferred_element_type=jnp.float32
    )
    whole_grad = lax.psum(local_grad, ("gx", "gy"))
    qkv_grad = lax.dynamic_slice_in_dim(
        whole_grad, lax.axis_index("gy") * shard_rows, shard_rows, 0
    )
    return (block_out, qkv_grad)


def solution(mesh):
    in_specs = (
        P("gx", "gy", None, None),
        P("gx", "gy", None, None),
        P(),
        P("gy", None),
        P("gy", None),
    )
    out_specs = (P("gx", "gy", None, None), P("gy", None))
    return jax.shard_map(shards, mesh=mesh, in_specs=in_specs, out_specs=out_specs, check_vma=False)
```

profile of v0, /device:TPU:0, one launch (start us, length us, event | category | flops | bytes accessed | tf_op | source)
XLA Modules:
  0.0 313.7 jit_solution(8115496946814767307)
XLA Ops:
  8.0 1.3 convert_reduce_fusion
  10.7 4.6 %collective-permute-start = (bf16[4,8,8,768]{3,2,1,0:T(8,128)(2,1)S(1)}, bf16[4,8,8,768]{3,2,1,0:T(8,128)(2,1)S(1)}, u32[]{:S(2)}, u32[]{:S(2)}) collective-permute-start(bf16[4,8,8,768]{3,2,1,0:T(8,128)(2,1)S(1)} %get-tuple-element.239), channel_id=1, source_target_pairs={{0,28},{4,0},{8,4},{12,8},{16,12},{20,16},{24,20},{28,24},{1,29},{... | collective-permute-start | bytes 1179656 | tf_op jit(solution)/shard_map/ppermute | solution.py:18
  15.3 5.3 %collective-permute-done = bf16[4,8,8,768]{3,2,1,0:T(8,128)(2,1)S(1)} collective-permute-done((bf16[4,8,8,768]{3,2,1,0:T(8,128)(2,1)S(1)}, bf16[4,8,8,768]{3,2,1,0:T(8,128)(2,1)S(1)}, u32[]{:S(2)}, u32[]{:S(2)}) %collective-permute-start) | collective-permute-done | bytes 393248 | tf_op jit(solution)/shard_map/ppermute | solution.py:18
  20.7 2.5 collective-permute-start.1
  23.2 18.8 %all_gather.7 = bf16[384,768]{1,0:T(8,128)(2,1)} all-gather(bf16[96,768]{1,0:T(8,128)(2,1)S(1)} %copy-done.3), channel_id=1, replica_groups=mesh['gx'=8,'gy'=4] {'gy'}, dimensions={0}, use_global_device_ids=true | all-gather | bytes 737280 | tf_op jit(solution)/shard_map/all_gather | solution.py:101
  42.0 13.0 %all-gather.2.cloned.1.call-done = bf16[768,1152]{1,0:T(8,128)(2,1)} async-done(((bf16[192,1152]{1,0:T(8,128)(2,1)}), bf16[768,1152]{1,0:T(8,128)(2,1)}) %all-gather.2.cloned.1.call-update) | async-done | bytes 1769488 | tf_op jit(solution)/shard_map/all_gather | solution.py:81
  55.0 2.7 fusion.43
  57.7 11.2 %while.30 = (s32[]{:T(128)}, bf16[1,512,384]{1,2,0:T(8,128)(2,1)S(1)}, bf16[1,512,1152]{2,1,0:T(8,128)(2,1)S(1)}, s32[]{:T(128)}, s32[]{:T(128)}, /*index=5*/s32...) while((s32[]{:T(128)}, bf16[1,512,384]{1,2,0:T(8,128)(2,1)S(1)}, ...), condition=%wide.region_5.6_spmd, body=%wide.region_2.5_spmd.sunk | while | flops 35404812 | bytes 3582236 | solution.py:95
  68.9 1.7 convolution_convert_fusion.3
  70.7 9.0 %collective-permute-done.2 = bf16[4,8,8,768]{3,2,1,0:T(8,128)(2,1)S(1)} collective-permute-done((bf16[4,8,8,768]{3,2,1,0:T(8,128)(2,1)S(1)}, bf16[4,8,8,768]{3,2,1,0:T(8,128)(2,1)S(1)}, u32[]{:S(2)}, u32[]{:S(2)}) %collective-permute-start.2) | collective-permute-done | bytes 393248 | tf_op jit(solution)/shard_map/ppermute | solution.py:18
  79.7 1.5 collective-permute-start.3
  81.3 7.8 %collective-permute-done.3 = bf16[8,4,8,768]{3,2,1,0:T(8,128)(2,1)S(1)} collective-permute-done((bf16[8,4,8,768]{3,2,1,0:T(8,128)(2,1)S(1)}, bf16[8,4,8,768]{3,2,1,0:T(8,128)(2,1)S(1)}, u32[]{:S(2)}, u32[]{:S(2)}) %collective-permute-start.3) | collective-permute-done | bytes 393248 | tf_op jit(solution)/shard_map/ppermute | solution.py:18
  90.3 1.5 multiply_convert_fusion.1
  92.5 5.3 %collective-permute-done.4 = bf16[4,8,8,768]{3,2,1,0:T(8,128)(2,1)S(1)} collective-permute-done((bf16[4,8,8,768]{3,2,1,0:T(8,128)(2,1)S(1)}, bf16[4,8,8,768]{3,2,1,0:T(8,128)(2,1)S(1)}, u32[]{:S(2)}, u32[]{:S(2)}) %collective-permute-start.4) | collective-permute-done | bytes 393248 | tf_op jit(solution)/shard_map/ppermute | solution.py:18
  98.5 10.7 %collective-permute-done.5 = bf16[8,4,8,768]{3,2,1,0:T(8,128)(2,1)} collective-permute-done((bf16[8,4,8,768]{3,2,1,0:T(8,128)(2,1)S(1)}, bf16[8,4,8,768]{3,2,1,0:T(8,128)(2,1)}, u32[]{:S(2)}, u32[]{:S(2)}) %collective-permute-start.5) | collective-permute-done | bytes 393248 | tf_op jit(solution)/shard_map/ppermute | solution.py:18
  109.2 1.1 pad_maximum_fusion.3
  110.9 1.1 broadcast_in_dim.25
  112.0 49.0 %while.31 = (s32[]{:T(128)}, bf16[1,512,1152]{1,2,0:T(8,128)(2,1)}, bf16[1,512,1152]{2,1,0:T(8,128)(2,1)S(1)}, bf16[1,512,384]{2,1,0:T(8,128)(2,1)S(1)}, s32[]{:...) while((s32[]{:T(128)}, bf16[1,512,1152]{1,2,0:T(8,128)(2,1)}, ...), condition=%wide.region_10.11_spmd, body=%wide.region_6.10_spmd.sunk | while | flops 88160776 | bytes 9951548 | solution.py:153
  134.6 1.0 fusion.101
  151.0 0.9 fusion.101
  159.1 0.9 fusion.101
  161.0 4.2 %fusion.50 = f32[768,1152]{1,0:T(8,128)} fusion(bf16[512,768]{1,0:T(8,128)(2,1)S(1)} %bitcast.110, bf16[1,512,1152]{1,2,0:T(8,128)(2,1)} %get-tuple-element.203), kind=kOutput, calls=%fused_computation.66 | convolution fusion | flops 905969664 | bytes 5505024 | tf_op jit(solution)/shard_map/dot_general | solution.py:162
  165.3 139.4 %all-reduce.2.cloned.1.call-done = f32[768,1152]{1,0:T(8,128)} async-done(((f32[768,1152]{1,0:T(8,128)}), f32[768,1152]{1,0:T(8,128)}) %all-reduce.2.cloned.1.call-update) | async-done | bytes 3538960 | tf_op jit(solution)/shard_map/psum | solution.py:165
  304.7 2.1 constant_dynamic-slice_fusion
  (152 shorter events, 62.7 us)
Async XLA Ops:
  7.2 2.1 copy-start
  7.2 2.5 copy-start.4
  7.2 47.9 %all-gather.2.cloned.1.call-start = ((), (), s32[]{:S(2)}) async-start(), calls=%async_computation | async-start | bytes 2211840 | tf_op jit(solution)/shard_map/all_gather | solution.py:81
  7.9 296.8 %all-reduce.2.cloned.1.call-start = ((), (), s32[]{:S(2)}) async-start(), calls=%async_computation.1 | async-start | bytes 7077888 | tf_op jit(solution)/shard_map/psum | solution.py:165
  10.7 12.5 %copy-start.3 = (bf16[96,768]{1,0:T(8,128)(2,1)S(1)}, bf16[96,768]{1,0:T(8,128)(2,1)}, u32[]{:S(2)}) copy-start(bf16[96,768]{1,0:T(8,128)(2,1)} %param.13) | copy-start | bytes 442372
  10.7 9.9 %collective-permute-start = (bf16[4,8,8,768]{3,2,1,0:T(8,128)(2,1)S(1)}, bf16[4,8,8,768]{3,2,1,0:T(8,128)(2,1)S(1)}, u32[]{:S(2)}, u32[]{:S(2)}) collective-permute-start(bf16[4,8,8,768]{3,2,1,0:T(8,128)(2,1)S(1)} %get-tuple-element.239), channel_id=1, source_target_pairs={{0,28},{4,0},{8,4},{12,8},{16,12},{20,16},{24,20},{28,24},{1,29},{... | collective-permute-start | bytes 1179656 | tf_op jit(solution)/shard_map/ppermute | solution.py:18
  20.7 21.3 %collective-permute-start.1 = (bf16[8,4,8,768]{3,2,1,0:T(8,128)(2,1)S(1)}, bf16[8,4,8,768]{3,2,1,0:T(8,128)(2,1)S(1)}, u32[]{:S(2)}, u32[]{:S(2)}) collective-permute-start(bf16[8,4,8,768]{3,2,1,0:T(8,128)(2,1)S(1)} %get-tuple-element.237), channel_id=1, source_target_pairs={{0,3},{1,0},{2,1},{3,2},{4,7},{5,4},{6,5},{7,6},{8,11},{9,8},{10,9... | collective-permute-start | bytes 1179656 | tf_op jit(solution)/shard_map/ppermute | solution.py:18
  70.7 9.1 %collective-permute-start.2 = (bf16[4,8,8,768]{3,2,1,0:T(8,128)(2,1)S(1)}, bf16[4,8,8,768]{3,2,1,0:T(8,128)(2,1)S(1)}, u32[]{:S(2)}, u32[]{:S(2)}) collective-permute-start(bf16[4,8,8,768]{3,2,1,0:T(8,128)(2,1)S(1)} %bitcast.114), channel_id=1, source_target_pairs={{0,4},{4,8},{8,12},{12,16},{16,20},{20,24},{24,28},{28,0},{1,5},{5... | collective-permute-start | bytes 1179656 | tf_op jit(solution)/shard_map/ppermute | solution.py:18
  79.7 9.3 %collective-permute-start.3 = (bf16[8,4,8,768]{3,2,1,0:T(8,128)(2,1)S(1)}, bf16[8,4,8,768]{3,2,1,0:T(8,128)(2,1)S(1)}, u32[]{:S(2)}, u32[]{:S(2)}) collective-permute-start(bf16[8,4,8,768]{3,2,1,0:T(8,128)(2,1)S(1)} %fusion.55), channel_id=1, source_target_pairs={{0,1},{1,2},{2,3},{3,0},{4,5},{5,6},{6,7},{7,4},{8,9},{9,10},{10,1... | collective-permute-start | bytes 1179656 | tf_op jit(solution)/shard_map/ppermute | solution.py:18
  89.1 1.1 copy-start.2
  92.5 5.4 %collective-permute-start.4 = (bf16[4,8,8,768]{3,2,1,0:T(8,128)(2,1)S(1)}, bf16[4,8,8,768]{3,2,1,0:T(8,128)(2,1)S(1)}, u32[]{:S(2)}, u32[]{:S(2)}) collective-permute-start(bf16[4,8,8,768]{3,2,1,0:T(8,128)(2,1)S(1)} %get-tuple-element.229), channel_id=1, source_target_pairs={{0,28},{4,0},{8,4},{12,8},{16,12},{20,16},{24,20},{28,24},{1,29},{... | collective-permute-start | bytes 1179656 | tf_op jit(solution)/shard_map/ppermute | solution.py:18
  97.9 12.4 %copy-start.1 = (bf16[384,768]{1,0:T(8,128)(2,1)S(1)}, bf16[384,768]{1,0:T(8,128)(2,1)}, u32[]{:S(2)}) copy-start(bf16[384,768]{1,0:T(8,128)(2,1)} %all_gather.7) | copy-start | bytes 1769476
  97.9 11.4 %collective-permute-start.5 = (bf16[8,4,8,768]{3,2,1,0:T(8,128)(2,1)S(1)}, bf16[8,4,8,768]{3,2,1,0:T(8,128)(2,1)}, u32[]{:S(2)}, u32[]{:S(2)}) collective-permute-start(bf16[8,4,8,768]{3,2,1,0:T(8,128)(2,1)S(1)} %get-tuple-element.227), channel_id=1, source_target_pairs={{0,3},{1,0},{2,1},{3,2},{4,7},{5,4},{6,5},{7,6},{8,11},{9,8},{10,9... | collective-permute-start | bytes 1179656 | tf_op jit(solution)/shard_map/ppermute | solution.py:18
Sparse Core Ops, SparseCore 0:
  9.8 45.1 all-gather.1
  165.4 139.2 all-reduce.1
where the time goes:
time: 314 us
  waiting for transfers between devices  191 us (61%)
  matrix products  60.9 us (19%)
  blocking collectives  18.8 us (6%)
  between operations  14.3 us (5%)
  other arithmetic  13.7 us (4%)
  starting transfers between devices  9.39 us (3%)
  local copies, waits for them, and re-layouts  5.15 us (2%)
    psum x1, waiting for transfers between devices, shards(): whole_grad = lax.psum(local_grad, ('gx', 'gy'))  139 us
    ppermute x6, waiting for transfers between devices, shifted(): lax.ppermute(x, axis, [(i, (i + by) % devices) for i in range(devices)])  38.1 us
    all_gather x1, blocking collectives, shards(): proj_whole = lax.all_gather(proj_weight, 'gy', axis=0, tiled=True)  18.8 us
    all_gather x1, waiting for transfers between devices, shards(): qkv_whole = lax.all_gather(qkv_weight, 'gy', axis=0, tiled=True)  13 us
    dot_general x12, matrix products, backward_head(): jnp.einsum('wqk,wqd->wkd', grad_scores, queries, preferred_element_type=j...  11.3 us
    dot_general x12, matrix products, backward_head(): jnp.einsum('wqk,wqd->wkd', prob_half, grad_mixed, preferred_element_type=...  11.2 us
    dot_general x12, matrix products, backward_head(): jnp.einsum('wqk,wkd->wqd', grad_scores, keys_in, preferred_element_type=j...  11 us
    dot_general x24, matrix products, head_probs(): jnp.einsum('wqd,wkd->wqk', queries, keys_in, preferred_element_type=jnp.f...  9.39 us
  transfers between devices with their start and end apart: 8, of which 7 were waited for; matrix products, arithmetic and copies ran while one was open for 1% of the time, Pallas kernels for 0%

commit v1 on v0

v1 whole, which is shorter than its diff:
```python
import functools
import math

import jax
import jax.numpy as jnp
from jax import lax
from jax.experimental import pallas as pl
from jax.experimental.pallas import tpu as pltpu
from jax.sharding import PartitionSpec as P

HEADS = 12
HD = 32
WIN = 8
HALF = WIN // 2
INNER = HEADS * HD
GROUPS = 3
GH = HEADS // GROUPS
GC = GH * HD
F32 = jnp.float32
BF16 = jnp.bfloat16
MESH = pl.DeviceIdType.MESH
norm_eps = 1e-05


def dot(a, b, ca, cb):
    return lax.dot_general(a, b, (((ca,), (cb,)), ((), ())), preferred_element_type=F32)


def flat_rows(x):
    rows = math.prod(x.shape[:-1])
    if x.shape[-2] % 16 == 0:
        return x.reshape(rows, x.shape[-1])
    return x.astype(F32).reshape(rows, x.shape[-1]).astype(BF16)


def kernel(
    nx, ny, scatter, loss_scale,
    tok, tgt, gain, wq, wp,
    out, grad,
    win, twin, wbuf, pbuf, xt, qkvt, ebuf, rinv, ot, blk, dot_t, dgrp,
    snd1, rcv1, s1, rcv2, snd3, rcv3, fin,
    ssem, rsem, lsem,
):
    nz = nx // 2
    x = lax.axis_index("gx")
    y = lax.axis_index("gy")
    core = lax.rem(x, 2)
    sib = x + 1 - 2 * core
    z = x // 2
    counter = [0]

    def gxi(d):
        return lax.rem(x + d + nx, nx)

    def gyi(d):
        return lax.rem(y + d + ny, ny)

    def remote(src, dst, dev):
        k = counter[0]
        counter[0] += 1
        return pltpu.make_async_remote_copy(
            src_ref=src, dst_ref=dst, send_sem=ssem.at[k], recv_sem=rsem.at[k],
            device_id=dev, device_id_type=MESH,
        )

    sent = []

    def go(copies):
        for c in copies:
            c.start()
            sent.append(c)

    peers = [(x, gyi(d)) for d in range(1, ny)]
    peers += [(gxi(1), y), (gxi(-1), y)]
    peers += [(gxi(2 * d), y) for d in range(1, nz)]
    peers += [(gxi(1), gyi(1)), (gxi(-1), gyi(-1))]
    barrier = pltpu.get_barrier_semaphore()
    for dev in peers:
        pl.semaphore_signal(barrier, inc=1, device_id=dev, device_id_type=MESH)
    locals_ = [
        pltpu.make_async_copy(tok.at[pl.ds(HALF, HALF), 1], win.at[0], lsem.at[0]),
        pltpu.make_async_copy(tgt.at[pl.ds(HALF, HALF), 1], twin.at[0], lsem.at[1]),
        pltpu.make_async_copy(wq, wbuf.at[y], lsem.at[2]),
        pltpu.make_async_copy(wp, pbuf.at[y], lsem.at[3]),
    ]
    for c in locals_:
        c.start()
    pl.semaphore_wait(barrier, len(peers))

    quarters = [(0, 1), (1, 0), (1, 1)]
    tok_copies = [
        remote(tok.at[pl.ds(HALF * (1 - a), HALF), 1 - b], win.at[2 * a + b], (gxi(-a), gyi(-b)))
        for a, b in quarters
    ]
    w_copies = [remote(wq.at[core], wbuf.at[y, core], (x, gyi(d))) for d in range(1, ny)]
    go(tok_copies)
    go(w_copies)

    def norm(q):
        v = win[q].reshape(-1, win.shape[-1]).astype(F32)
        mean = jnp.mean(v, -1, keepdims=True)
        cen = v - mean
        var = jnp.mean(cen * cen, -1, keepdims=True)
        nrm = cen * lax.rsqrt(var + norm_eps) * gain[...]
        rows = v.shape[0]
        xt[:, q * rows:(q + 1) * rows] = nrm.T.astype(BF16)

    locals_[0].wait()
    norm(0)
    w_fwd = []
    for d in range(1, ny):
        w_copies[d - 1].wait_recv()
        owner = gyi(-d)
        w_fwd.append(remote(wbuf.at[owner, core], wbuf.at[owner, core], (sib, y)))
        go(w_fwd[-1:])
    for (a, b), c in zip(quarters, tok_copies):
        c.wait_recv()
        norm(2 * a + b)
    p_copies = [remote(wp, pbuf.at[y], (x, gyi(d))) for d in range(1, ny)]
    t_copies = [
        remote(tgt.at[pl.ds(HALF * (1 - a), HALF), 1 - b], twin.at[2 * a + b], (gxi(-a), gyi(-b)))
        for a, b in quarters
    ]
    go(p_copies)
    go(t_copies)
    for c in w_fwd:
        c.wait_recv()
    locals_[2].wait()
    qkvt[...] = dot(flat_rows(wbuf[...]), xt[...], 0, 0).astype(BF16)

    scale = HD ** (-0.5)
    c2 = scale * math.log2(math.e)

    def rows_of(h, base=0):
        return pl.ds(pl.multiple_of(base + h * HD, HD), HD)

    def fwd(h, carry):
        q = qkvt[rows_of(h), :]
        k = qkvt[rows_of(h, INNER), :]
        v = qkvt[rows_of(h, 2 * INNER), :]
        s = dot(k, q, 0, 0)
        m = jnp.max(s, 0, keepdims=True)
        e = jnp.exp2((s - m) * c2)
        r = 1.0 / jnp.sum(e, 0, keepdims=True)
        eb = e.astype(BF16)
        ebuf[h] = eb
        rinv[h] = r
        ot[rows_of(h), :] = dot(v, eb, 1, 0) * r
        return carry

    lax.fori_loop(0, HEADS, fwd, 0)

    for c in p_copies:
        c.wait_recv()
    locals_[3].wait()
    proj = flat_rows(pbuf[...])
    res = dot(ot[...].astype(BF16), proj, 0, 0).astype(BF16)
    blk[...] = res.reshape(blk.shape)
    o_copies = [
        remote(blk.at[2 * a + b], out.at[pl.ds(HALF * (1 - a), HALF), 1 - b], (gxi(a), gyi(b)))
        for a, b in quarters
    ]
    go(o_copies)
    own = pltpu.make_async_copy(blk.at[0], out.at[pl.ds(HALF, HALF), 1], lsem.at[4])
    own.start()
    for c in t_copies:
        c.wait_recv()
    locals_[1].wait()
    tw = twin[...].reshape(res.shape)
    g = ((res.astype(F32) - tw.astype(F32)) * loss_scale).astype(BF16)
    dot_t[...] = dot(proj, g, 1, 1).astype(BF16)

    def bwd(h, g0):
        q = qkvt[rows_of(h), :]
        k = qkvt[rows_of(h, INNER), :]
        v = qkvt[rows_of(h, 2 * INNER), :]
        eb = ebuf[h]
        do = dot_t[rows_of(h), :].astype(F32) * rinv[h]
        dob = do.astype(BF16)
        rd = jnp.sum(do * ot[rows_of(h), :], 0, keepdims=True)
        dp = dot(v, dob, 0, 0)
        ds = (eb.astype(F32) * (dp - rd)).astype(BF16)
        hl = h - g0
        dgrp[rows_of(hl), :] = (dot(k, ds, 1, 0) * scale).astype(BF16)
        dgrp[rows_of(hl, GC), :] = (dot(q, ds, 1, 1) * scale).astype(BF16)
        dgrp[rows_of(hl, 2 * GC), :] = dot(dob, eb, 1, 1).astype(BF16)

    def half_group(i):
        per = GH // 2
        g0 = (i // 2) * GH

        def body(t, carry):
            bwd(i * per + t, g0)
            return carry

        lax.fori_loop(0, per, body, 0)

    st = {}

    def stage_a(i):
        dw = dot(xt[...], dgrp[...], 1, 1)
        hr = snd1.shape[3]
        dw = dw.reshape(ny, 2, hr, 3 * GC).astype(BF16)
        for cc in range(2):
            snd1[i, cc] = dw[:, cc]
        st["a", i] = [remote(snd1.at[i, 1 - core], rcv1.at[i], (sib, y))]
        go(st["a", i])

    def stage_b(i):
        for c in st["a", i]:
            c.wait_recv()
        s1[i] = (snd1[i, core].astype(F32) + rcv1[i].astype(F32)).astype(BF16)
        st["b", i] = [
            remote(s1.at[i, gyi(d)], rcv2.at[i, d - 1], (x, gyi(d))) for d in range(1, ny)
        ]
        go(st["b", i])

    def stage_c(i):
        acc = s1[i, y].astype(F32)
        for d in range(1, ny):
            st["b", i][d - 1].wait_recv()
            acc = acc + rcv2[i, d - 1].astype(F32)
        snd3[i] = acc.reshape(snd3.shape[1:]).astype(BF16)
        copies = []
        for d in range(1, nz):
            piece = lax.rem(z + d, nz) if scatter else 0
            copies.append(remote(snd3.at[i, piece], rcv3.at[i, d - 1], (gxi(2 * d), y)))
        st["c", i] = copies
        go(copies)

    def stage_d(i):
        piece = z if scatter else 0
        acc = snd3[i, piece].astype(F32)
        for d in range(1, nz):
            st["c", i][d - 1].wait_recv()
            acc = acc + rcv3[i, d - 1].astype(F32)
        fin[i, core, piece] = acc.astype(BF16)
        st["d", i] = []
        if scatter:
            st["d", i] = [
                remote(fin.at[i, core, z], fin.at[i, core, z], (gxi(2 * d), y))
                for d in range(1, nz)
            ]
            go(st["d", i])

    def stage_e(i):
        for c in st["d", i]:
            c.wait_recv()
        st["e", i] = [remote(fin.at[i, core], fin.at[i, core], (sib, y))]
        go(st["e", i])

    def stage_f(i):
        for c in st["e", i]:
            c.wait_recv()
        res = fin[i].astype(F32).reshape(grad.shape[0], 3 * GC)
        for part in range(3):
            lo = part * INNER + i * GC
            grad[:, lo:lo + GC] = res[:, part * GC:(part + 1) * GC]

    half_group(0)
    half_group(1)
    stage_a(0)
    half_group(2)
    stage_b(0)
    half_group(3)
    stage_a(1)
    stage_c(0)
    half_group(4)
    stage_b(1)
    half_group(5)
    stage_a(2)
    stage_d(0)
    stage_c(1)
    stage_b(2)
    stage_e(0)
    stage_d(1)
    stage_c(2)
    stage_f(0)
    stage_e(1)
    stage_d(2)
    stage_f(1)
    stage_e(2)
    stage_f(2)
    for c in o_copies:
        c.wait_recv()
    own.wait()
    for c in sent:
        c.wait_send()


def shards(nx, ny, tokens, target, norm_gain, qkv_weight, proj_weight):
    ex, ey, ez, ch = tokens.shape
    rows = HALF * ez
    wr = qkv_weight.shape[0]
    pr = proj_weight.shape[0]
    hr = wr // 2
    nz = nx // 2
    scatter = hr % (8 * nz) == 0
    pieces = nz if scatter else 1
    prow = hr // pieces
    n_tok = ex * ey * ez
    inner3 = qkv_weight.shape[1]
    gw = inner3 // GROUPS
    loss_scale = 2.0 / math.sqrt(n_tok * nx * ny)
    ncopies = 9 + 3 * (ny - 1) + GROUPS * (2 + (ny - 1) + (nz - 1) * (2 if scatter else 1))
    any_spec = pl.BlockSpec(memory_space=pl.ANY)
    vm_spec = pl.BlockSpec(memory_space=pltpu.VMEM)
    block, grad = pl.pallas_call(
        functools.partial(kernel, nx, ny, scatter, loss_scale),
        out_shape=(
            jax.ShapeDtypeStruct((ex, 2, rows, ch), BF16),
            jax.ShapeDtypeStruct((wr, inner3), F32),
        ),
        in_specs=[any_spec, any_spec, vm_spec, any_spec, any_spec],
        out_specs=(any_spec, vm_spec),
        scratch_shapes=[
            pltpu.VMEM((4, HALF, rows, ch), BF16),
            pltpu.VMEM((4, HALF, rows, ch), BF16),
            pltpu.VMEM((ny, 2, hr, inner3), BF16),
            pltpu.VMEM((ny, pr, ch), BF16),
            pltpu.VMEM((ch, n_tok), BF16),
            pltpu.VMEM((inner3, n_tok), BF16),
            pltpu.VMEM((HEADS, n_tok, n_tok), BF16),
            pltpu.VMEM((HEADS, 1, n_tok), F32),
            pltpu.VMEM((INNER, n_tok), F32),
            pltpu.VMEM((4, HALF, rows, ch), BF16),
            pltpu.VMEM((INNER, n_tok), BF16),
            pltpu.VMEM((gw, n_tok), BF16),
            pltpu.VMEM((GROUPS, 2, ny, hr, gw), BF16),
            pltpu.VMEM((GROUPS, ny, hr, gw), BF16),
            pltpu.VMEM((GROUPS, ny, hr, gw), BF16),
            pltpu.VMEM((GROUPS, ny - 1, hr, gw), BF16),
            pltpu.VMEM((GROUPS, pieces, prow, gw), BF16),
            pltpu.VMEM((GROUPS, nz - 1, prow, gw), BF16),
            pltpu.VMEM((GROUPS, 2, pieces, prow, gw), BF16),
            pltpu.SemaphoreType.DMA((ncopies,)),
            pltpu.SemaphoreType.DMA((ncopies,)),
            pltpu.SemaphoreType.DMA((5,)),
        ],
        compiler_params=pltpu.CompilerParams(
            collective_id=0, has_side_effects=True, vmem_limit_bytes=60 * 2**20
        ),
        name="step",
    )(
        tokens.reshape(ex, 2, rows, ch),
        target.reshape(ex, 2, rows, ch),
        norm_gain.reshape(1, ch),
        qkv_weight.reshape(2, hr, inner3),
        proj_weight,
    )
    return block.reshape(ex, ey, ez, ch), grad


def solution(mesh):
    nx, ny = mesh.shape["gx"], mesh.shape["gy"]
    in_specs = (
        P("gx", "gy", None, None),
        P("gx", "gy", None, None),
        P(),
        P("gy", None),
        P("gy", None),
    )
    out_specs = (P("gx", "gy", None, None), P("gy", None))
    return jax.shard_map(
        functools.partial(shards, nx, ny),
        mesh=mesh, in_specs=in_specs, out_specs=out_specs, check_vma=False,
    )
```

time: 314 us -> 86.2 us (0.27)
  waiting for transfers between devices: 191 us -> 0 us
  Pallas kernels: 0 us -> 81 us
  matrix products: 60.9 us -> 0 us
  blocking collectives: 18.8 us -> 0 us
  other arithmetic: 13.7 us -> 0 us
  between operations: 14.3 us -> 0.66 us
  starting transfers between devices: 9.39 us -> 0 us
    psum x1 -> x0, waiting for transfers between devices: 139 us -> none  [shards(): whole_grad = lax.psum(local_grad, ('gx', 'gy'))]
    pallas_call x0 -> x1, Pallas kernels: none -> 81 us  [shards(): pl.pallas_call(functools.partial(kernel, nx, ny, scatter, loss_scale), ou...]
    dot_general x88 -> x0, matrix products: 60.9 us -> none  [the longest x12 11.3 us: backward_head(): jnp.einsum('wqk,wqd->wkd', grad_scores, queries, preferred_element_type=j...]
    ppermute x6 -> x0, waiting for transfers between devices: 38.1 us -> none  [shifted(): lax.ppermute(x, axis, [(i, (i + by) % devices) for i in range(devices)])]
    all_gather x1 -> x0, blocking collectives: 18.8 us -> none  [shards(): proj_whole = lax.all_gather(proj_weight, 'gy', axis=0, tiled=True)]
    all_gather x1 -> x0, waiting for transfers between devices: 13 us -> none  [shards(): qkv_whole = lax.all_gather(qkv_weight, 'gy', axis=0, tiled=True)]
    ppermute x6 -> x0, starting transfers between devices: 9.31 us -> none  [shifted(): lax.ppermute(x, axis, [(i, (i + by) % devices) for i in range(devices)])]
    reduce_sum x26 -> x0, other arithmetic: 6.37 us -> none  [the longest x24 4.71 us: head_probs(): return exponent / jnp.sum(exponent, -1, keepdims=True)]
  transfers between devices with their start and end apart: 8 -> 0, of which waited for: 7 -> 0; matrix products, arithmetic and copies ran while one was open for 1% -> 0% of each run, Pallas kernels for 0% -> 0%
where the time goes in v1:
time: 86.2 us; the launch traced here: 86 us
  Pallas kernels  81 us (94%)
  local copies, waits for them, and re-layouts  4.32 us (5%)
    pallas_call x1, Pallas kernels, shards(): pl.pallas_call(functools.partial(kernel, nx, ny, scatter, loss_scale), ou...  81 us
    unnamed x6, local copies, waits for them, and re-layouts  3.74 us

profile of v1, /device:TPU:0, one launch (start us, length us, event | category | flops | bytes accessed | tf_op | source)
XLA Modules:
  0.0 86.0 jit_solution(3554313525875476390)
XLA Ops:
  0.6 0.0 copy-start.1
  0.6 0.7 copy-done.1
  1.3 0.6 reshape.21.gain
  1.9 81.0 %step.1 = (bf16[8,2,32,768]{3,2,1,0:T(8,128)(2,1)}, f32[192,1152]{1,0:T(8,128)}) custom-call(bf16[8,2,32,768]{3,2,1,0:T(8,128)(2,1)} %bitcast.4, bf16[8,2,32,768]{3,2,1,0:T(8,128)(2,1)} %bitcast.5, f32[1,768]{1,0:T(1,128)} %reshape.21.gain, bf16[2,96,1152]{2,1,0:T(8,128)(2,1)} %bitcast.7, bf16[96,768]{1,0:T(8,128)(2,1)} %wp.1), custom_call_target="tpu_custom_call" | custom-call | tf_op jit(solution)/shard_map/step/pallas_call | solution.py:308
  82.9 0.0 copy-start
  82.9 2.1 %copy.9 = bf16[8,8,8,768]{3,2,1,0:T(8,128)(2,1)} copy(bf16[8,8,8,768]{3,2,1,0:T(8,128)(2,1)} %bitcast.6) | data formatting | bytes 1572864
  85.1 0.0 copy-done
  85.1 0.9 %copy.10 = f32[192,1152]{1,0:T(8,128)} copy(f32[192,1152]{1,0:T(8,128)S(1)} %copy-done) | data formatting | bytes 1769472
Async XLA Ops:
  0.6 0.7 copy-start.1
  82.9 2.2 %copy-start = (f32[192,1152]{1,0:T(8,128)S(1)}, f32[192,1152]{1,0:T(8,128)}, u32[]{:S(2)}) copy-start(f32[192,1152]{1,0:T(8,128)} %get-tuple-element.9) | copy-start | bytes 2654212

commit v2 on v1

--- a/solution.py
+++ b/solution.py
@@ -34,10 +34,10 @@
 
 
 def kernel(
-    nx, ny, scatter, loss_scale,
+    nx, ny, scatter, wsplit, psplit, loss_scale,
     tok, tgt, gain, wq, wp,
     out, grad,
-    win, twin, wbuf, pbuf, xt, qkvt, ebuf, rinv, ot, blk, dot_t, dgrp,
+    win, thome, tph, tpw, aw, ah, wbuf, pbuf, xt, qkvt, ebuf, rinv, ot, dot_t, dgrp,
     snd1, rcv1, s1, rcv2, snd3, rcv3, fin,
     ssem, rsem, lsem,
 ):
@@ -47,6 +47,11 @@
     core = lax.rem(x, 2)
     sib = x + 1 - 2 * core
     z = x // 2
+    zodd = lax.rem(z, 2)
+    zmate = x + 2 - 4 * zodd
+    wpart = core + 2 * zodd if wsplit == 4 else core
+    zpart = core + 2 * (1 - zodd)
+    ppart = core if psplit == 2 else 0
     counter = [0]
 
     def gxi(d):
@@ -79,7 +84,7 @@
         pl.semaphore_signal(barrier, inc=1, device_id=dev, device_id_type=MESH)
     locals_ = [
         pltpu.make_async_copy(tok.at[pl.ds(HALF, HALF), 1], win.at[0], lsem.at[0]),
-        pltpu.make_async_copy(tgt.at[pl.ds(HALF, HALF), 1], twin.at[0], lsem.at[1]),
+        pltpu.make_async_copy(tgt, thome, lsem.at[1]),
         pltpu.make_async_copy(wq, wbuf.at[y], lsem.at[2]),
         pltpu.make_async_copy(wp, pbuf.at[y], lsem.at[3]),
     ]
@@ -92,38 +97,47 @@
         remote(tok.at[pl.ds(HALF * (1 - a), HALF), 1 - b], win.at[2 * a + b], (gxi(-a), gyi(-b)))
         for a, b in quarters
     ]
-    w_copies = [remote(wq.at[core], wbuf.at[y, core], (x, gyi(d))) for d in range(1, ny)]
+    w_copies = [remote(wq.at[wpart], wbuf.at[y, wpart], (x, gyi(d))) for d in range(1, ny)]
+    p_copies = [remote(wp.at[ppart], pbuf.at[y, ppart], (x, gyi(d))) for d in range(1, ny)]
+    go(w_copies)
     go(tok_copies)
-    go(w_copies)
+    go(p_copies)
 
     def norm(q):
         v = win[q].reshape(-1, win.shape[-1]).astype(F32)
         mean = jnp.mean(v, -1, keepdims=True)
         cen = v - mean
         var = jnp.mean(cen * cen, -1, keepdims=True)
-        nrm = cen * lax.rsqrt(var + norm_eps) * gain[...]
+        nrm = cen * lax.rsqrt(var + norm_eps) * gain[...].reshape(1, -1)
         rows = v.shape[0]
         xt[:, q * rows:(q + 1) * rows] = nrm.T.astype(BF16)
 
     locals_[0].wait()
     norm(0)
-    w_fwd = []
+    w_sib = []
+    w_z = []
     for d in range(1, ny):
         w_copies[d - 1].wait_recv()
-        owner = gyi(-d)
-        w_fwd.append(remote(wbuf.at[owner, core], wbuf.at[owner, core], (sib, y)))
-        go(w_fwd[-1:])
-    for (a, b), c in zip(quarters, tok_copies):
-        c.wait_recv()
-        norm(2 * a + b)
-    p_copies = [remote(wp, pbuf.at[y], (x, gyi(d))) for d in range(1, ny)]
-    t_copies = [
-        remote(tgt.at[pl.ds(HALF * (1 - a), HALF), 1 - b], twin.at[2 * a + b], (gxi(-a), gyi(-b)))
-        for a, b in quarters
-    ]
-    go(p_copies)
-    go(t_copies)
-    for c in w_fwd:
+        mine = wbuf.at[gyi(-d), wpart]
+        if wsplit == 4:
+            w_z.append(remote(mine, mine, (zmate, y)))
+            go(w_z[-1:])
+        w_sib.append(remote(mine, mine, (sib, y)))
+        go(w_sib[-1:])
+    order = [1, 0, 2]
+    for t in order[:1]:
+        tok_copies[t].wait_recv()
+        norm(t + 1)
+    for d in range(1, ny):
+        if wsplit == 4:
+            w_z[d - 1].wait_recv()
+            other = wbuf.at[gyi(-d), zpart]
+            w_sib.append(remote(other, other, (sib, y)))
+            go(w_sib[-1:])
+    for t in order[1:]:
+        tok_copies[t].wait_recv()
+        norm(t + 1)
+    for c in w_sib:
         c.wait_recv()
     locals_[2].wait()
     qkvt[...] = dot(flat_rows(wbuf[...]), xt[...], 0, 0).astype(BF16)
@@ -148,27 +162,47 @@
         ot[rows_of(h), :] = dot(v, eb, 1, 0) * r
         return carry
 
-    lax.fori_loop(0, HEADS, fwd, 0)
-
-    for c in p_copies:
+    p_sib = []
+    for d in range(1, ny):
+        p_copies[d - 1].wait_recv()
+        if psplit == 2:
+            mine = pbuf.at[gyi(-d), ppart]
+            p_sib.append(remote(mine, mine, (sib, y)))
+            go(p_sib[-1:])
+    lax.fori_loop(0, GH // 2, fwd, 0)
+    for c in p_sib:
         c.wait_recv()
     locals_[3].wait()
+    locals_[1].wait()
     proj = flat_rows(pbuf[...])
-    res = dot(ot[...].astype(BF16), proj, 0, 0).astype(BF16)
-    blk[...] = res.reshape(blk.shape)
+    n_tok = xt.shape[1]
+    tph[...] = dot(thome[...].reshape(n_tok, -1), proj, 1, 1).astype(BF16).reshape(tph.shape)
+    t_copies = [
+        remote(tph.at[pl.ds(HALF * (1 - a), HALF), 1 - b], tpw.at[2 * a + b], (gxi(-a), gyi(-b)))
+        for a, b in quarters
+    ]
+    go(t_copies)
+    own_t = pltpu.make_async_copy(tph.at[pl.ds(HALF, HALF), 1], tpw.at[0], lsem.at[4])
+    own_t.start()
+    lax.fori_loop(GH // 2, HEADS, fwd, 0)
+
+    attn = ot[...].T.astype(BF16)
+    aw[...] = attn.reshape(aw.shape)
     o_copies = [
-        remote(blk.at[2 * a + b], out.at[pl.ds(HALF * (1 - a), HALF), 1 - b], (gxi(a), gyi(b)))
+        remote(aw.at[2 * a + b], ah.at[pl.ds(HALF * (1 - a), HALF), 1 - b], (gxi(a), gyi(b)))
         for a, b in quarters
     ]
     go(o_copies)
-    own = pltpu.make_async_copy(blk.at[0], out.at[pl.ds(HALF, HALF), 1], lsem.at[4])
-    own.start()
+    own_a = pltpu.make_async_copy(aw.at[0], ah.at[pl.ds(HALF, HALF), 1], lsem.at[5])
+    own_a.start()
+    proj = flat_rows(pbuf[...])
+    res = dot(attn, proj, 1, 0).astype(BF16)
+    back = dot(res, proj, 1, 1)
     for c in t_copies:
         c.wait_recv()
-    locals_[1].wait()
-    tw = twin[...].reshape(res.shape)
-    g = ((res.astype(F32) - tw.astype(F32)) * loss_scale).astype(BF16)
-    dot_t[...] = dot(proj, g, 1, 1).astype(BF16)
+    own_t.wait()
+    tw = tpw[...].reshape(n_tok, -1).astype(F32)
+    dot_t[...] = ((back - tw) * loss_scale).T.astype(BF16)
 
     def bwd(h, g0):
         q = qkvt[rows_of(h), :]
@@ -252,7 +286,7 @@
     def stage_f(i):
         for c in st["e", i]:
             c.wait_recv()
-        res = fin[i].astype(F32).reshape(grad.shape[0], 3 * GC)
+        res = flat_rows(fin[i])
         for part in range(3):
             lo = part * INNER + i * GC
             grad[:, lo:lo + GC] = res[:, part * GC:(part + 1) * GC]
@@ -271,6 +305,11 @@
     stage_a(2)
     stage_d(0)
     stage_c(1)
+    for c in o_copies:
+        c.wait_recv()
+    own_a.wait()
+    home = ah[...].reshape(n_tok, -1)
+    out[...] = dot(home, flat_rows(pbuf[...]), 1, 0).astype(BF16)
     stage_b(2)
     stage_e(0)
     stage_d(1)
@@ -281,11 +320,13 @@
     stage_f(1)
     stage_e(2)
     stage_f(2)
-    for c in o_copies:
-        c.wait_recv()
-    own.wait()
     for c in sent:
         c.wait_send()
+
+
+def finish(b_in, g_in, b_out, g_out):
+    b_out[...] = b_in[...]
+    g_out[...] = g_in[...].astype(F32)
 
 
 def shards(nx, ny, tokens, target, norm_gain, qkv_weight, proj_weight):
@@ -293,6 +334,8 @@
     rows = HALF * ez
     wr = qkv_weight.shape[0]
     pr = proj_weight.shape[0]
+    wsplit = 4 if wr % 64 == 0 else 2
+    psplit = 2 if pr % 32 == 0 else 1
     hr = wr // 2
     nz = nx // 2
     scatter = hr % (8 * nz) == 0
@@ -302,28 +345,31 @@
     inner3 = qkv_weight.shape[1]
     gw = inner3 // GROUPS
     loss_scale = 2.0 / math.sqrt(n_tok * nx * ny)
-    ncopies = 9 + 3 * (ny - 1) + GROUPS * (2 + (ny - 1) + (nz - 1) * (2 if scatter else 1))
+    ncopies = 9 + 6 * (ny - 1) + GROUPS * (2 + (ny - 1) + (nz - 1) * (2 if scatter else 1))
     any_spec = pl.BlockSpec(memory_space=pl.ANY)
     vm_spec = pl.BlockSpec(memory_space=pltpu.VMEM)
     block, grad = pl.pallas_call(
-        functools.partial(kernel, nx, ny, scatter, loss_scale),
+        functools.partial(kernel, nx, ny, scatter, wsplit, psplit, loss_scale),
         out_shape=(
-            jax.ShapeDtypeStruct((ex, 2, rows, ch), BF16),
-            jax.ShapeDtypeStruct((wr, inner3), F32),
+            jax.ShapeDtypeStruct((n_tok, ch), BF16),
+            jax.ShapeDtypeStruct((wr, inner3), BF16),
         ),
         in_specs=[any_spec, any_spec, vm_spec, any_spec, any_spec],
-        out_specs=(any_spec, vm_spec),
+        out_specs=(vm_spec, vm_spec),
         scratch_shapes=[
             pltpu.VMEM((4, HALF, rows, ch), BF16),
-            pltpu.VMEM((4, HALF, rows, ch), BF16),
-            pltpu.VMEM((ny, 2, hr, inner3), BF16),
-            pltpu.VMEM((ny, pr, ch), BF16),
+            pltpu.VMEM((ex, 2, rows, ch), BF16),
+            pltpu.VMEM((ex, 2, rows, INNER), BF16),
+            pltpu.VMEM((4, HALF, rows, INNER), BF16),
+            pltpu.VMEM((4, HALF, rows, INNER), BF16),
+            pltpu.VMEM((ex, 2, rows, INNER), BF16),
+            pltpu.VMEM((ny, wsplit, wr // wsplit, inner3), BF16),
+            pltpu.VMEM((ny, psplit, pr // psplit, ch), BF16),
             pltpu.VMEM((ch, n_tok), BF16),
             pltpu.VMEM((inner3, n_tok), BF16),
             pltpu.VMEM((HEADS, n_tok, n_tok), BF16),
             pltpu.VMEM((HEADS, 1, n_tok), F32),
             pltpu.VMEM((INNER, n_tok), F32),
-            pltpu.VMEM((4, HALF, rows, ch), BF16),
             pltpu.VMEM((INNER, n_tok), BF16),
             pltpu.VMEM((gw, n_tok), BF16),
             pltpu.VMEM((GROUPS, 2, ny, hr, gw), BF16),
@@ -335,7 +381,7 @@
             pltpu.VMEM((GROUPS, 2, pieces, prow, gw), BF16),
             pltpu.SemaphoreType.DMA((ncopies,)),
             pltpu.SemaphoreType.DMA((ncopies,)),
-            pltpu.SemaphoreType.DMA((5,)),
+            pltpu.SemaphoreType.DMA((6,)),
         ],
         compiler_params=pltpu.CompilerParams(
             collective_id=0, has_side_effects=True, vmem_limit_bytes=60 * 2**20
@@ -344,10 +390,24 @@
     )(
         tokens.reshape(ex, 2, rows, ch),
         target.reshape(ex, 2, rows, ch),
-        norm_gain.reshape(1, ch),
-        qkv_weight.reshape(2, hr, inner3),
-        proj_weight,
+        norm_gain,
+        qkv_weight.reshape(wsplit, wr // wsplit, inner3),
+        proj_weight.reshape(psplit, pr // psplit, ch),
     )
+    steps = 4 if wr % 64 == 0 else 1
+    bspec = pl.BlockSpec((n_tok // steps, ch), lambda i: (i, 0))
+    gspec = pl.BlockSpec((wr // steps, inner3), lambda i: (i, 0))
+    block, grad = pl.pallas_call(
+        finish,
+        grid=(steps,),
+        out_shape=(
+            jax.ShapeDtypeStruct(block.shape, BF16),
+            jax.ShapeDtypeStruct(grad.shape, F32),
+        ),
+        in_specs=[bspec, gspec],
+        out_specs=(bspec, gspec),
+        name="finish",
+    )(block, grad)
     return block.reshape(ex, ey, ez, ch), grad
 
 

time: 86.2 us -> 77 us (0.89)
  Pallas kernels: 81 us -> 76.2 us
  local copies, waits for them, and re-layouts: 4.32 us -> 0 us
    pallas_call x1 -> x2, Pallas kernels: 81 us -> 76.2 us  [the longest x1 72.6 us: shards(): pl.pallas_call(functools.partial(kernel, nx, ny, scatter, wsplit, psplit,...]
    unnamed x6 -> x0, local copies, waits for them, and re-layouts: 3.74 us -> none
where the time goes in v2:
time: 77 us; the launch traced here: 76.8 us
  Pallas kernels  76.2 us (99%)
    pallas_call x1, Pallas kernels, shards(): pl.pallas_call(functools.partial(kernel, nx, ny, scatter, wsplit, psplit,...  72.6 us
    pallas_call x1, Pallas kernels, shards(): pl.pallas_call(finish, grid=(steps,), out_shape=(jax.ShapeDtypeStruct(blo...  3.57 us

profile of v2, /device:TPU:0, one launch (start us, length us, event | category | flops | bytes accessed | tf_op | source)
XLA Modules:
  0.0 76.8 jit_solution(12317304764204098824)
XLA Ops:
  0.6 72.6 %step.1 = (bf16[512,768]{1,0:T(8,128)(2,1)}, bf16[192,1152]{1,0:T(8,128)(2,1)}) custom-call(bf16[8,2,32,768]{3,2,1,0:T(8,128)(2,1)} %bitcast.5, bf16[8,2,32,768]{3,2,1,0:T(8,128)(2,1)} %bitcast.6, f32[768]{0:T(1024)} %gain.1, bf16[4,48,1152]{2,1,0:T(8,128)(2,1)} %bitcast.7, bf16[2,48,768]{2,1,0:T(8,128)(2,1)} %bitcast.8), custom_call_target="tpu_custom_call" | custom-call | tf_op jit(solution)/shard_map/step/pallas_call | solution.py:351
  73.2 3.6 %finish.1 = (bf16[512,768]{1,0:T(8,128)(2,1)}, f32[192,1152]{1,0:T(8,128)}) custom-call(bf16[512,768]{1,0:T(8,128)(2,1)} %get-tuple-element.6.b_in, bf16[192,1152]{1,0:T(8,128)(2,1)} %get-tuple-element.7.g_in), custom_call_target="tpu_custom_call" | custom-call | tf_op jit(solution)/shard_map/finish/pallas_call | solution.py:400
